TPU v7x, 32 devices: a whole 2x2x4 slice. The times are simulated.
32 devices in a mesh: grp: 8 (over z, x), hd: 4 (over y, core).
Axes of the slice: x: 2, y: 2, z: 4, core: 2. Of those that a mesh axis runs over, the one named last changes fastest.
Arguments:
- query_states: bfloat16 [4096, 2048], P(('grp', 'hd')), may hold values from -8 to 8
- key_states: bfloat16 [4096, 2048], P(('grp', 'hd')), may hold values from -8 to 8
- value_states: bfloat16 [4096, 2048], P(('grp', 'hd')), may hold values from -6 to 6
- output_cotangent: bfloat16 [4096, 2048], P(('grp', 'hd')), may hold values from -6 to 6
- pattern: int32 [32, 2], replicated, may hold values from 0 to 31, as said below
Outputs:
- attended: bfloat16 [4096, 2048], P(('grp', 'hd'))
- query_gradient: bfloat16 [4096, 2048], P(('grp', 'hd'))
- key_gradient: bfloat16 [4096, 2048], P(('grp', 'hd'))
- value_gradient: bfloat16 [4096, 2048], P(('grp', 'hd'))
Inputs may be any that keep to these rules, and one draw needn't show every extreme that they name: `pattern`: random columns never name a block of the query's own group. The random columns of one query group name exactly 4 distinct blocks. Counting the window blocks next to the group and the random blocks together, a query group names at most 2 distinct blocks of any one other group, and exactly 2 of some group.
All inputs are finite; a program needn't handle non-finite values.
Results may differ from a plain program's by a relative error of at most 0.01.
Values may be sent and summed in bfloat16 or wider, within the bound.
A program may use at most 128 MiB of HBM per device.

v0:
```python
import math

import jax
import jax.numpy as jnp
from jax import lax
from jax.sharding import PartitionSpec as P

HEADS = 16
HEAD_DIM = 128
BLOCK = 128
GLOBALS = 1
RANDOM = 2


mask_value = -1e30


def spread_2(array, axis, root):
    mine = lax.axis_index(axis) == root
    return lax.psum(jnp.where(mine, array, jnp.zeros_like(array)), axis)


def take_rows(source, first_row, row_count):
    return lax.dynamic_slice_in_dim(source, first_row, row_count, 0)


def block_scores(query_part, key_part, valid_part, score_scale):
    scores = (
        jnp.einsum("qthd,qkshd->qhtks", query_part, key_part, preferred_element_type=jnp.float32)
        * score_scale
    )
    scores = jnp.where(valid_part[:, None, None, :, None], scores, mask_value)
    return scores.reshape(scores.shape[0], scores.shape[1], scores.shape[2], -1)


def on_device(query_states, key_states, value_states, output_cotangent, pattern):
    groups_count = lax.axis_size("grp")
    head_groups = lax.axis_size("hd")
    group_index = lax.axis_index("grp")
    local_heads = HEADS // head_groups
    head_width = local_heads * HEAD_DIM
    pair_width = 2 * head_width
    group_tokens = query_states.shape[0] * head_groups
    group_blocks = group_tokens // BLOCK
    all_blocks = group_blocks * groups_count
    pool_size = group_blocks * RANDOM // 2
    capacity = max(2, (2 * pool_size + 4) // groups_count)
    slot_count = groups_count * capacity
    key_count = 3 + GLOBALS + RANDOM
    step_blocks = min(group_blocks, max(1, 512 // BLOCK))
    step_count = group_blocks // step_blocks
    score_scale = 1.0 / math.sqrt(HEAD_DIM)
    query_heads, key_heads, value_heads, cotangent_heads = (
        lax.all_to_all(query_states, "hd", split_axis=1, concat_axis=0, tiled=True),
        lax.all_to_all(key_states, "hd", split_axis=1, concat_axis=0, tiled=True),
        lax.all_to_all(value_states, "hd", split_axis=1, concat_axis=0, tiled=True),
        lax.all_to_all(output_cotangent, "hd", split_axis=1, concat_axis=0, tiled=True),
    )
    query_blocks = query_heads.reshape(group_blocks, BLOCK, local_heads, HEAD_DIM)
    pair_blocks = jnp.concatenate([key_heads, value_heads], axis=1).reshape(
        group_blocks, BLOCK, pair_width
    )
    global_pairs = spread_2(pair_blocks[:GLOBALS], "grp", 0)
    first_block = group_index * group_blocks
    block_ids = jnp.arange(all_blocks, dtype=jnp.int32)
    own_rows = lax.dynamic_slice_in_dim(pattern, first_block, group_blocks, 0)
    wanted = jnp.any(own_rows.reshape(-1, 1) == block_ids[None, :], axis=0)
    wanted = wanted | (block_ids == first_block - 1) | (block_ids == first_block + group_blocks)
    wanted = wanted & (block_ids // group_blocks != group_index)
    rank_in = (
        jnp.cumsum(wanted.reshape(groups_count, group_blocks).astype(jnp.int32), axis=1) - 1
    ).reshape(-1)
    every_rows = pattern.reshape(groups_count, group_blocks * RANDOM)
    own_blocks = first_block + jnp.arange(group_blocks, dtype=jnp.int32)
    requested = jnp.any(every_rows[:, :, None] == own_blocks[None, None, :], axis=1)
    dest_ids = jnp.arange(groups_count, dtype=jnp.int32)[:, None]
    local_ids = jnp.arange(group_blocks, dtype=jnp.int32)[None, :]
    requested = (
        requested
        | (dest_ids == group_index + 1) & (local_ids == group_blocks - 1)
        | (dest_ids == group_index - 1) & (local_ids == 0)
    )
    requested = requested & (dest_ids != group_index)
    rank_out = jnp.cumsum(requested.astype(jnp.int32), axis=1) - 1
    selector = (
        requested[:, None, :]
        & (rank_out[:, None, :] == jnp.arange(capacity, dtype=jnp.int32)[None, :, None])
    ).astype(jnp.bfloat16)
    outgoing = jnp.einsum(
        "gcj,jtx->gctx", selector, pair_blocks, preferred_element_type=jnp.float32
    ).astype(jnp.bfloat16)
    incoming = lax.all_to_all(outgoing, "grp", split_axis=0, concat_axis=0, tiled=True)
    slot_pairs = incoming.reshape(slot_count, BLOCK, pair_width)
    random_slots = own_rows // group_blocks * capacity + rank_in[own_rows]
    left_slot = jnp.clip(
        (group_index - 1) * capacity + rank_in[jnp.maximum(first_block - 1, 0)], 0, slot_count - 1
    )
    right_slot = jnp.clip(
        (group_index + 1) * capacity
        + rank_in[jnp.minimum(first_block + group_blocks, all_blocks - 1)],
        0,
        slot_count - 1,
    )
    left_pairs = jnp.concatenate([slot_pairs[left_slot][None], pair_blocks[:-1]], axis=0)
    right_pairs = jnp.concatenate([pair_blocks[1:], slot_pairs[right_slot][None]], axis=0)
    random_pairs = slot_pairs[random_slots]
    query_ids = first_block + jnp.arange(group_blocks, dtype=jnp.int32)
    valid_keys = jnp.concatenate(
        [
            (query_ids >= 1)[:, None],
            jnp.ones((group_blocks, 1), jnp.bool_),
            (query_ids + 1 < all_blocks)[:, None],
            jnp.ones((group_blocks, GLOBALS + RANDOM), jnp.bool_),
        ],
        axis=1,
    )

    def assemble(first_row):
        window = jnp.stack(
            [
                take_rows(left_pairs, first_row, step_blocks),
                take_rows(pair_blocks, first_row, step_blocks),
                take_rows(right_pairs, first_row, step_blocks),
            ],
            axis=1,
        )
        spread = jnp.broadcast_to(global_pairs[None], (step_blocks, GLOBALS, BLOCK, pair_width))
        return jnp.concatenate(
            [window, spread, take_rows(random_pairs, first_row, step_blocks)], axis=1
        )

    def split_pairs(pair_part):
        key_part = pair_part[..., :head_width].reshape(
            step_blocks, key_count, BLOCK, local_heads, HEAD_DIM
        )
        value_part = pair_part[..., head_width:].reshape(
            step_blocks, key_count * BLOCK, local_heads, HEAD_DIM
        )
        return (key_part, value_part)

    def forward_step(loop_state, step_index):
        first_row = step_index * step_blocks
        key_part, value_part = split_pairs(assemble(first_row))
        scores = block_scores(
            take_rows(query_blocks, first_row, step_blocks),
            key_part,
            take_rows(valid_keys, first_row, step_blocks),
            score_scale,
        )
        row_peaks = jnp.max(scores, axis=-1, keepdims=True)
        weights = jnp.exp(scores - row_peaks)
        totals = jnp.sum(weights, axis=-1, keepdims=True)
        soft_weights = (weights / totals).astype(jnp.bfloat16)
        attended = jnp.einsum(
            "qhtn,qnhd->qthd", soft_weights, value_part, preferred_element_type=jnp.float32
        ).astype(jnp.bfloat16)
        stored = (attended, row_peaks, totals, soft_weights)
        return (loop_state, stored)

    scan_state, forward_out = lax.scan(forward_step, 0, jnp.arange(step_count))
    cotangent_blocks = cotangent_heads.reshape(group_blocks, BLOCK, local_heads, HEAD_DIM)

    def backward_step(global_sum, step_index):
        first_row = step_index * step_blocks
        key_part, value_part = split_pairs(assemble(first_row))
        key_flat = key_part.reshape(step_blocks, key_count * BLOCK, local_heads, HEAD_DIM)
        query_part = take_rows(query_blocks, first_row, step_blocks)
        soft_weights = forward_out[3][step_index]
        cotangent_part = take_rows(cotangent_blocks, first_row, step_blocks)
        attended_part = forward_out[0][step_index]
        row_delta = jnp.sum(
            cotangent_part.astype(jnp.float32) * attended_part.astype(jnp.float32), axis=-1
        )
        row_delta = jnp.transpose(row_delta, (0, 2, 1))[..., None]
        prob_grad = jnp.einsum(
            "qthd,qnhd->qhtn", cotangent_part, value_part, preferred_element_type=jnp.float32
        )
        score_grad = (
            soft_weights.astype(jnp.float32) * (prob_grad - row_delta) * score_scale
        ).astype(jnp.bfloat16)
        query_grad = jnp.einsum(
            "qhtn,qnhd->qthd", score_grad, key_flat, preferred_element_type=jnp.float32
        ).astype(jnp.bfloat16)
        key_terms = jnp.einsum(
            "qhtn,qthd->qnhd", score_grad, query_part, preferred_element_type=jnp.float32
        )
        value_terms = jnp.einsum(
            "qhtn,qthd->qnhd", soft_weights, cotangent_part, preferred_element_type=jnp.float32
        )
        entry_terms = jnp.concatenate(
            [
                key_terms.reshape(step_blocks, key_count, BLOCK, head_width),
                value_terms.reshape(step_blocks, key_count, BLOCK, head_width),
            ],
            axis=-1,
        )
        global_sum = global_sum + jnp.sum(entry_terms[:, 3 : 3 + GLOBALS], axis=0)
        return (global_sum, (query_grad, entry_terms[:, :3], entry_terms[:, 3 + GLOBALS :]))

    global_sum, backward_out = lax.scan(
        backward_step, jnp.zeros((GLOBALS, BLOCK, pair_width), jnp.float32), jnp.arange(step_count)
    )
    query_grads = backward_out[0].reshape(group_tokens, head_width)
    window_terms = backward_out[1].reshape(group_blocks, 3, BLOCK, pair_width)
    random_terms = backward_out[2].reshape(group_blocks * RANDOM, BLOCK * pair_width)
    slot_select = (
        random_slots.reshape(1, -1) == jnp.arange(slot_count, dtype=jnp.int32)[:, None]
    ).astype(jnp.float32)
    slot_sum = jnp.dot(slot_select, random_terms, precision=lax.Precision.HIGHEST).reshape(
        slot_count, BLOCK, pair_width
    )
    slot_sum = (
        slot_sum.at[left_slot]
        .add(window_terms[0, 0])
        .at[right_slot]
        .add(window_terms[group_blocks - 1, 2])
    )
    zero_block = jnp.zeros((1, BLOCK, pair_width), jnp.float32)
    local_grads = (
        window_terms[:, 1]
        + jnp.concatenate([window_terms[1:, 0], zero_block], axis=0)
        + jnp.concatenate([zero_block, window_terms[:-1, 2]], axis=0)
    )
    returned = lax.all_to_all(
        slot_sum.astype(jnp.bfloat16).reshape(groups_count, capacity, BLOCK, pair_width),
        "grp",
        split_axis=0,
        concat_axis=0,
        tiled=True,
    )
    local_grads = local_grads + jnp.einsum(
        "gcj,gctx->jtx", selector, returned, preferred_element_type=jnp.float32
    )
    global_total = lax.psum(global_sum, "grp")
    local_grads = local_grads.at[:GLOBALS].add(jnp.where(group_index == 0, global_total, 0.0))
    key_grads = local_grads[..., :head_width].reshape(group_tokens, head_width).astype(jnp.bfloat16)
    value_grads = (
        local_grads[..., head_width:].reshape(group_tokens, head_width).astype(jnp.bfloat16)
    )
    attended_heads = forward_out[0].reshape(group_tokens, head_width)
    return (
        lax.all_to_all(attended_heads, "hd", split_axis=0, concat_axis=1, tiled=True),
        lax.all_to_all(query_grads, "hd", split_axis=0, concat_axis=1, tiled=True),
        lax.all_to_all(key_grads, "hd", split_axis=0, concat_axis=1, tiled=True),
        lax.all_to_all(value_grads, "hd", split_axis=0, concat_axis=1, tiled=True),
    )


def solution(mesh):
    return jax.shard_map(
        on_device,
        mesh=mesh,
        in_specs=(
            P(("grp", "hd"), None),
            P(("grp", "hd"), None),
            P(("grp", "hd"), None),
            P(("grp", "hd"), None),
            P(),
        ),
        out_specs=(
            P(("grp", "hd"), None),
            P(("grp", "hd"), None),
            P(("grp", "hd"), None),
            P(("grp", "hd"), None),
        ),
        check_vma=False,
    )
```

profile of v0, /device:TPU:0, one launch (start us, length us, event | category | flops | bytes accessed | tf_op | source)
XLA Modules:
  0.0 520.2 jit_solution(13643224141856430011)
XLA Ops:
  9.5 4.3 all-to-all-start
  17.2 5.4 %all-to-all-done = bf16[128,4,512]{2,0,1:T(8,128)(2,1)S(1)} async-done(((bf16[128,4,512]{2,0,1:T(8,128)(2,1)}), bf16[128,4,512]{2,0,1:T(8,128)(2,1)S(1)}, u32[]{:S(2)}, u32[]{:S(2)}) %all-to-all-start) | async-done | bytes 524320 | tf_op jit(solution)/shard_map/all_to_all | solution.py:55
  26.6 8.2 %all-to-all-done.1 = bf16[128,4,512]{2,0,1:T(8,128)(2,1)S(1)} async-done(((bf16[128,4,512]{2,0,1:T(8,128)(2,1)}), bf16[128,4,512]{2,0,1:T(8,128)(2,1)S(1)}, u32[]{:S(2)}, u32[]{:S(2)}) %all-to-all-start.1) | async-done | bytes 524320 | tf_op jit(solution)/shard_map/all_to_all | solution.py:56
  37.1 4.3 copy.141
  41.5 6.6 %all-to-all-start.2 = ((bf16[8,2,128,1024]{3,2,1,0:T(8,128)(2,1)}), bf16[8,2,128,1024]{3,2,1,0:T(8,128)(2,1)}, u32[]{:S(2)}, u32[]{:S(2)}) async-start(bf16[8,2,128,1024]{3,2,1,0:T(8,128)(2,1)} %copy.141), calls=%async_computation.2 | async-start | bytes 8388608 | tf_op jit(solution)/shard_map/all_to_all | solution.py:92
  57.2 88.1 %all-to-all-done.2 = bf16[8,2,128,1024]{3,2,1,0:T(8,128)(2,1)} async-done(((bf16[8,2,128,1024]{3,2,1,0:T(8,128)(2,1)}), bf16[8,2,128,1024]{3,2,1,0:T(8,128)(2,1)}, u32[]{:S(2)}, u32[]{:S(2)}) %all-to-all-start.2) | async-done | bytes 4194336 | tf_op jit(solution)/shard_map/all_to_all | solution.py:92
  158.0 24.1 %all-reduce.5.cloned.1.call-done = bf16[128,1024]{1,0:T(8,128)(2,1)} async-done(((bf16[128,1024]{1,0:T(8,128)(2,1)}), bf16[128,1024]{1,0:T(8,128)(2,1)}) %all-reduce.5.cloned.1.call-update) | async-done | bytes 262160 | tf_op jit(solution)/shard_map/psum | solution.py:20
  185.8 5.2 fusion.72
  193.8 4.4 all-to-all-start.5
  205.3 5.5 %reshape.397 = bf16[4,768,4,128]{3,2,1,0:T(4,128)(2,1)} reshape(bf16[4,6,128,512]{3,2,1,0:T(8,128)(2,1)} %get-tuple-element.130) | data formatting | bytes 6291456 | tf_op jit(solution)/shard_map/while/body/eval_jaxpr/reshape | solution.py:136
  210.9 5.8 %convolution_bitcast_fusion = f32[4,768,4,128]{3,1,2,0:T(8,128)} fusion(bf16[4,4,128,768]{2,3,1,0:T(8,128)(2,1)} %fusion.2, bf16[4,128,4,128]{1,3,2,0:T(8,128)(2,1)} %bitcast.34), kind=kOutput, calls=%fused_computation.25 | convolution fusion | flops 402653184 | bytes 9961472 | tf_op jit(solution)/shard_map/while/body/eval_jaxpr/qhtn,qthd->qnhd/dot_general | solution.py:187
  224.8 6.7 %copy.193 = f32[4,768,4,128]{3,2,0,1:T(4,128)} copy(f32[4,768,4,128]{3,1,2,0:T(8,128)S(1)} %convolution_bitcast_fusion.1) | data formatting | bytes 12582912 | tf_op jit(solution)/shard_map/while/body/eval_jaxpr/reshape | solution.py:192
  231.4 8.6 %reshape.435 = f32[4,6,128,512]{3,0,2,1:T(4,128)} reshape(f32[4,768,4,128]{3,2,0,1:T(4,128)} %copy.193) | data formatting | bytes 12582912 | tf_op jit(solution)/shard_map/while/body/eval_jaxpr/reshape | solution.py:192
  240.1 9.5 %copy.194 = f32[4,768,4,128]{3,2,0,1:T(4,128)} copy(f32[4,768,4,128]{3,1,2,0:T(8,128)} %convolution_bitcast_fusion) | data formatting | bytes 12582912 | tf_op jit(solution)/shard_map/while/body/eval_jaxpr/reshape | solution.py:193
  249.5 8.3 %reshape.436 = f32[4,6,128,512]{3,0,2,1:T(4,128)} reshape(f32[4,768,4,128]{3,2,0,1:T(4,128)} %copy.194) | data formatting | bytes 12582912 | tf_op jit(solution)/shard_map/while/body/eval_jaxpr/reshape | solution.py:193
  257.8 4.8 constant_dynamic-update-slice_fusion.2
  262.6 5.1 constant_dynamic-update-slice_fusion.1
  271.2 5.5 %fusion.43 = f32[16,128,1024]{2,0,1:T(8,128)S(1)} fusion(s32[8]{0:T(128)S(1)} %eq.136, f32[1,8,128,1024]{3,2,1,0:T(8,128)S(1)} %bitcast.160), kind=kOutput, calls=%fused_computation.78 | convolution fusion | flops 201326720 | bytes 12582944 | tf_op jit(solution)/shard_map/dot_general | solution.py:209
  282.1 11.0 %scatter-add.10 = f32[16,128,1024]{2,0,1:T(8,128)} dynamic-update-slice(f32[16,128,1024]{2,0,1:T(8,128)} %copy-done, f32[1,128,1024]{2,0,1:T(1,128)} %broadcast_select_fusion.2, s32[]{:T(128)} %min.14, s32[]{:T(128)} %constant.182.clone.1, s32[]{:T(128)} %constant.182.clone.1) | dynamic-update-slice | bytes 1048580 | tf_op jit(solution)/shard_map/scatter-add | solution.py:214
  293.1 5.1 broadcast_select_fusion.1
  298.3 11.0 %scatter-add.11 = f32[16,128,1024]{2,0,1:T(8,128)} dynamic-update-slice(f32[16,128,1024]{2,0,1:T(8,128)} %scatter-add.10, f32[1,128,1024]{2,0,1:T(1,128)} %broadcast_select_fusion.1, s32[]{:T(128)} %min.16, s32[]{:T(128)} %constant.182.clone.1, s32[]{:T(128)} %constant.182.clone.1) | dynamic-update-slice | bytes 1048580 | tf_op jit(solution)/shard_map/scatter-add | solution.py:216
  309.3 6.1 %convert_element_type.68 = bf16[16,128,1024]{2,0,1:T(8,128)(2,1)} convert(f32[16,128,1024]{2,0,1:T(8,128)} %scatter-add.11) | non-fusion elementwise | flops 2097152 | bytes 12582912 | tf_op jit(solution)/shard_map/convert_element_type | solution.py:225
  315.4 7.4 %reshape.408 = bf16[8,2,128,1024]{3,1,0,2:T(2,128)(2,1)} reshape(bf16[16,128,1024]{2,0,1:T(8,128)(2,1)} %convert_element_type.68) | data formatting | bytes 8388608 | tf_op jit(solution)/shard_map/reshape | solution.py:225
  322.8 7.0 %copy.170 = bf16[8,2,128,1024]{3,1,2,0:T(2,128)(2,1)} copy(bf16[8,2,128,1024]{3,1,0,2:T(2,128)(2,1)} %reshape.408) | data formatting | bytes 8388608 | tf_op jit(solution)/shard_map/reshape | solution.py:225
  329.9 4.6 all-to-all-start.7
  341.3 5.5 %slice_bitcast_fusion.1 = (f32[3,128,1024]{2,0,1:T(4,128)}, f32[3,128,1024]{2,0,1:T(4,128)}) fusion(f32[4,6,128,1024]{3,0,2,1:T(4,128)} %copy-done.1), kind=kLoop, calls=%fused_computation.29 | loop fusion | bytes 6291456 | tf_op jit(solution)/shard_map/squeeze | solution.py:221
  348.7 87.1 %all-to-all-done.7 = bf16[8,2,128,1024]{3,1,2,0:T(2,128)(2,1)} async-done(((bf16[8,2,128,1024]{3,1,2,0:T(2,128)(2,1)}), bf16[8,2,128,1024]{3,1,2,0:T(2,128)(2,1)}, u32[]{:S(2)}, u32[]{:S(2)}) %all-to-all-start.7) | async-done | bytes 4194336 | tf_op jit(solution)/shard_map/all_to_all | solution.py:224
  439.3 7.6 %fusion.23 = f32[4,128,1024]{2,0,1:T(4,128)S(1)} fusion(f32[4,6,128,1024]{3,0,2,1:T(4,128)} %copy-done.1, f32[3,128,1024]{2,0,1:T(4,128)} %get-tuple-element.129, f32[3,128,1024]{2,0,1:T(4,128)} %get-tuple-element.128, bf16[8,2,128,1024]{3,1,2,0:T(2,128)(2,1)} %all-to-all-done.7, s32[8,4]{0,1:T(4,128)S(1)} %broadcast_add_fusion.1, ...), kind=kOutput, calls=%fused_computation.33 | convolution fusion | flops 18350208 | bytes 11534496 | tf_op jit(solution)/shard_map/gcj,gctx->jtx/dot_general | solution.py:231
  451.9 22.7 %all-reduce.7.cloned.1.call-done = f32[1,128,1024]{2,0,1:T(1,128)} async-done(((f32[1,128,1024]{2,0,1:T(1,128)}), f32[1,128,1024]{2,0,1:T(1,128)}) %all-reduce.7.cloned.1.call-update) | async-done | bytes 524304 | tf_op jit(solution)/shard_map/psum | solution.py:234
  477.1 8.3 %scatter-add.14 = f32[4,128,1024]{2,0,1:T(4,128)S(1)} dynamic-update-slice(f32[4,128,1024]{2,0,1:T(4,128)S(1)} %fusion.23, f32[1,128,1024]{2,0,1:T(1,128)} %fusion.38, s32[]{:T(128)} %constant.182.clone.1, s32[]{:T(128)} %constant.182.clone.1, s32[]{:T(128)} %constant.182.clone.1) | dynamic-update-slice | bytes 1048580 | tf_op jit(solution)/shard_map/scatter-add | solution.py:235
  491.5 7.9 %all-to-all-done.9 = bf16[4,128,512]{2,1,0:T(8,128)(2,1)S(1)} async-done(((bf16[4,128,512]{2,1,0:T(8,128)(2,1)}), bf16[4,128,512]{2,1,0:T(8,128)(2,1)S(1)}, u32[]{:S(2)}, u32[]{:S(2)}) %all-to-all-start.9) | async-done | bytes 524320 | tf_op jit(solution)/shard_map/all_to_all | solution.py:245
  506.2 5.5 %all-to-all-done.8 = bf16[4,128,512]{2,1,0:T(8,128)(2,1)S(1)} async-done(((bf16[4,128,512]{2,1,0:T(8,128)(2,1)}), bf16[4,128,512]{2,1,0:T(8,128)(2,1)S(1)}, u32[]{:S(2)}, u32[]{:S(2)}) %all-to-all-start.8) | async-done | bytes 524320 | tf_op jit(solution)/shard_map/all_to_all | solution.py:244
  (115 shorter events, 96.9 us)
Async XLA Ops:
  9.5 13.1 %all-to-all-start = ((bf16[128,4,512]{2,0,1:T(8,128)(2,1)}), bf16[128,4,512]{2,0,1:T(8,128)(2,1)S(1)}, u32[]{:S(2)}, u32[]{:S(2)}) async-start(bf16[128,4,512]{2,0,1:T(8,128)(2,1)} %copy.136), calls=%async_computation | async-start | bytes 1048576 | tf_op jit(solution)/shard_map/all_to_all | solution.py:55
  22.6 12.3 %all-to-all-start.1 = ((bf16[128,4,512]{2,0,1:T(8,128)(2,1)}), bf16[128,4,512]{2,0,1:T(8,128)(2,1)S(1)}, u32[]{:S(2)}, u32[]{:S(2)}) async-start(bf16[128,4,512]{2,0,1:T(8,128)(2,1)} %copy.139), calls=%async_computation.1 | async-start | bytes 1048576 | tf_op jit(solution)/shard_map/all_to_all | solution.py:56
  41.5 10.4 %copy-start.7 = (bf16[128,2048]{1,0:T(8,128)(2,1)S(1)}, bf16[128,2048]{1,0:T(8,128)(2,1)}, u32[]{:S(2)}) copy-start(bf16[128,2048]{1,0:T(8,128)(2,1)} %param.11) | copy-start | bytes 1572868
  41.5 11.4 %copy-start.8 = (bf16[128,2048]{1,0:T(8,128)(2,1)S(1)}, bf16[128,2048]{1,0:T(8,128)(2,1)}, u32[]{:S(2)}) copy-start(bf16[128,2048]{1,0:T(8,128)(2,1)} %param.14) | copy-start | bytes 1572868
  41.5 103.8 %all-to-all-start.2 = ((bf16[8,2,128,1024]{3,2,1,0:T(8,128)(2,1)}), bf16[8,2,128,1024]{3,2,1,0:T(8,128)(2,1)}, u32[]{:S(2)}, u32[]{:S(2)}) async-start(bf16[8,2,128,1024]{3,2,1,0:T(8,128)(2,1)} %copy.141), calls=%async_computation.2 | async-start | bytes 8388608 | tf_op jit(solution)/shard_map/all_to_all | solution.py:92
  48.1 5.8 %copy-start.9 = (s32[3]{0:T(128)S(1)}, s32[3]{0:T(128)}, u32[]{:S(2)}) copy-start(s32[3]{0:T(128)} %constant.195.clone.1) | copy-start | bytes 40
  48.1 134.0 %all-reduce.5.cloned.1.call-start = ((), (), s32[]{:S(2)}) async-start(), calls=%async_computation.10 | async-start | bytes 524288 | tf_op jit(solution)/shard_map/psum | solution.py:20
  145.3 48.5 %all-to-all-start.3 = ((bf16[128,4,512]{0,2,1:T(8,128)(2,1)}), bf16[128,4,512]{0,2,1:T(8,128)(2,1)}, u32[]{:S(2)}, u32[]{:S(2)}) async-start(bf16[128,4,512]{0,2,1:T(8,128)(2,1)} %bitcast.176), calls=%async_computation.3 | async-start | bytes 1048576 | tf_op jit(solution)/shard_map/all_to_all | solution.py:54
  193.8 17.1 %all-to-all-start.5 = ((bf16[128,4,512]{0,2,1:T(8,128)(2,1)}), bf16[128,4,512]{0,2,1:T(8,128)(2,1)}, u32[]{:S(2)}, u32[]{:S(2)}) async-start(bf16[128,4,512]{0,2,1:T(8,128)(2,1)} %bitcast.175), calls=%async_computation.5 | async-start | bytes 1048576 | tf_op jit(solution)/shard_map/all_to_all | solution.py:57
  210.9 5.8 %copy-start.2 = (bf16[4,4,128,768]{2,3,1,0:T(8,128)(2,1)S(1)}, bf16[4,4,128,768]{2,3,1,0:T(8,128)(2,1)}, u32[]{:S(2)}) copy-start(bf16[4,4,128,768]{2,3,1,0:T(8,128)(2,1)} %fusion.2) | copy-start | bytes 9437188
  210.9 5.8 %copy-start.6 = (bf16[4,768,4,128]{3,2,1,0:T(4,128)(2,1)S(1)}, bf16[4,768,4,128]{3,2,1,0:T(4,128)(2,1)}, u32[]{:S(2)}) copy-start(bf16[4,768,4,128]{3,2,1,0:T(4,128)(2,1)} %reshape.397) | copy-start | bytes 9437188
  222.3 2.4 copy-start.3
  267.8 8.9 %copy-start.1 = (f32[4,6,128,1024]{3,0,2,1:T(4,128)}, f32[4,6,128,1024]{3,0,2,1:T(4,128)S(1)}, u32[]{:S(2)}) copy-start(f32[4,6,128,1024]{3,0,2,1:T(4,128)S(1)} %constant_dynamic-update-slice_fusion.1) | copy-start | bytes 37748740
  276.7 3.3 copy-start
  329.9 106.0 %all-to-all-start.7 = ((bf16[8,2,128,1024]{3,1,2,0:T(2,128)(2,1)}), bf16[8,2,128,1024]{3,1,2,0:T(2,128)(2,1)}, u32[]{:S(2)}, u32[]{:S(2)}) async-start(bf16[8,2,128,1024]{3,1,2,0:T(2,128)(2,1)} %copy.170), calls=%async_computation.7 | async-start | bytes 8388608 | tf_op jit(solution)/shard_map/all_to_all | solution.py:224
  334.4 140.1 %all-reduce.7.cloned.1.call-start = ((), (), s32[]{:S(2)}) async-start(), calls=%async_computation.11 | async-start | bytes 1048576 | tf_op jit(solution)/shard_map/psum | solution.py:234
  341.3 5.6 %copy-start.4 = (bf16[4,4,128,768]{2,3,1,0:T(8,128)(2,1)S(1)}, bf16[4,4,128,768]{2,3,1,0:T(8,128)(2,1)}, u32[]{:S(2)}) copy-start(bf16[4,4,128,768]{2,3,1,0:T(8,128)(2,1)} %copy-done.3) | copy-start | bytes 9437188
  341.3 5.6 %copy-start.5 = (bf16[4,768,4,128]{3,2,1,0:T(4,128)(2,1)S(1)}, bf16[4,768,4,128]{3,2,1,0:T(4,128)(2,1)}, u32[]{:S(2)}) copy-start(bf16[4,768,4,128]{3,2,1,0:T(4,128)(2,1)} %reshape.401) | copy-start | bytes 9437188
  435.9 12.3 %all-to-all-start.4 = ((bf16[4,128,512]{1,2,0:T(8,128)(2,1)}), bf16[4,128,512]{1,2,0:T(8,128)(2,1)S(1)}, u32[]{:S(2)}, u32[]{:S(2)}) async-start(bf16[4,128,512]{1,2,0:T(8,128)(2,1)} %bitcast.29), calls=%async_computation.4 | async-start | bytes 1048576 | tf_op jit(solution)/shard_map/all_to_all | solution.py:242
  448.1 39.0 %all-to-all-start.6 = ((bf16[4,128,512]{1,2,0:T(8,128)(2,1)}), bf16[4,128,512]{1,2,0:T(8,128)(2,1)S(1)}, u32[]{:S(2)}, u32[]{:S(2)}) async-start(bf16[4,128,512]{1,2,0:T(8,128)(2,1)} %bitcast.183), calls=%async_computation.6 | async-start | bytes 1048576 | tf_op jit(solution)/shard_map/all_to_all | solution.py:243
  487.2 12.3 %all-to-all-start.9 = ((bf16[4,128,512]{2,1,0:T(8,128)(2,1)}), bf16[4,128,512]{2,1,0:T(8,128)(2,1)S(1)}, u32[]{:S(2)}, u32[]{:S(2)}) async-start(bf16[4,128,512]{2,1,0:T(8,128)(2,1)} %copy.174), calls=%async_computation.9 | async-start | bytes 1048576 | tf_op jit(solution)/shard_map/all_to_all | solution.py:245
  499.4 12.3 %all-to-all-start.8 = ((bf16[4,128,512]{2,1,0:T(8,128)(2,1)}), bf16[4,128,512]{2,1,0:T(8,128)(2,1)S(1)}, u32[]{:S(2)}, u32[]{:S(2)}) async-start(bf16[4,128,512]{2,1,0:T(8,128)(2,1)} %copy.172), calls=%async_computation.8 | async-start | bytes 1048576 | tf_op jit(solution)/shard_map/all_to_all | solution.py:244
Sparse Core Ops, SparseCore 0:
  55.8 126.2 all-reduce.4
  341.4 133.1 all-reduce.6
where the time goes:
time: 530 us; the launch traced here: 520 us
  waiting for transfers between devices  250 us (47%)
  local copies, waits for them, and re-layouts  148 us (28%)
  starting transfers between devices  41.7 us (8%)
  matrix products  34.3 us (6%)
  other arithmetic  29.5 us (6%)
  between operations  16.2 us (3%)
    all_to_all x1, waiting for transfers between devices, on_device(): lax.all_to_all(outgoing, 'grp', split_axis=0, concat_axis=0, tiled=True)  88.1 us
    all_to_all x1, waiting for transfers between devices, on_device(): lax.all_to_all(slot_sum.astype(jnp.bfloat16).reshape(groups_count, capaci...  87.1 us
    psum x1, waiting for transfers between devices, spread_2(): return lax.psum(jnp.where(mine, array, jnp.zeros_like(array)), axis)  24.1 us
    psum x1, waiting for transfers between devices, on_device(): global_total = lax.psum(global_sum, 'grp')  22.7 us
    scatter-add x2, local copies, waits for them, and re-layouts, on_device(): slot_sum = slot_sum.at[left_slot].add(window_terms[0, 0]).at[right_slot]....  22.1 us
    unnamed x29, local copies, waits for them, and re-layouts  17.9 us
    reshape x2, local copies, waits for them, and re-layouts, backward_step(): value_terms.reshape(step_blocks, key_count, BLOCK, head_width)  17.7 us
    reshape x2, local copies, waits for them, and re-layouts, backward_step(): key_terms.reshape(step_blocks, key_count, BLOCK, head_width)  15.3 us
  transfers between devices with their start and end apart: 12, of which 9 were waited for; matrix products, arithmetic and copies ran while one was open for 16% of the time, Pallas kernels for 0%

commit v1 on v0

v1 whole, which is shorter than its diff:
```python
import functools
import math

import jax
import jax.numpy as jnp
from jax import lax
from jax.experimental import pallas as pl
from jax.experimental.pallas import tpu as pltpu
from jax.sharding import PartitionSpec as P

HEADS = 16
HEAD_DIM = 128
BLOCK = 128
GLOBALS = 1
RANDOM = 2
MASK_VALUE = -1e30
VMEM_BYTES = 60 * 1024 * 1024
MESH = pl.DeviceIdType.MESH


def place(team, hd_size):
    index = lax.axis_index("grp") * hd_size + lax.axis_index("hd")
    return index // team, index % team


def target(number, hd_size):
    return (number // hd_size, number % hd_size)


def far_first(step):
    return 1 + (HEADS // 2 - 1 + step) % (HEADS - 1)


def enter(head, member, team, hd_size):
    barrier = pltpu.get_barrier_semaphore()

    def greet(number):
        pl.semaphore_signal(barrier, inc=1, device_id=target(number, hd_size), device_id_type=MESH)

    @pl.loop(1, HEADS)
    def _(step):
        greet((head + step) % HEADS * team + member)

    @pl.loop(1, team)
    def _(step):
        greet(head * team + (member + step) % team)

    pl.semaphore_wait(barrier, HEADS - 1 + team - 1)


def columns(head):
    return pl.ds(pl.multiple_of(head * HEAD_DIM, HEAD_DIM), HEAD_DIM)


def gather_kernel(
    team, hd_size, q_in, k_in, v_in, g_in, q_out, k_out, v_out, g_out,
    send_sem, recv_sem, own_sem, pass_send, pass_recv,
):
    head, member = place(team, hd_size)
    enter(head, member, team, hd_size)
    arrays = (
        (k_in, lambda at: k_out.at[at, member]),
        (v_in, lambda at: v_out.at[at, member]),
        (q_in, lambda at: q_out.at[at]),
        (g_in, lambda at: g_out.at[at]),
    )

    def remote(number, peer):
        source, dest = arrays[number]
        return pltpu.make_async_remote_copy(
            source.at[:, columns(peer)], dest(head), send_sem.at[number, peer],
            recv_sem.at[number, head], device_id=target(peer * team + member, hd_size),
            device_id_type=MESH,
        )

    def arrival(number, peer):
        source, dest = arrays[number]
        return pltpu.make_async_remote_copy(
            source.at[:, columns(peer)], dest(peer), send_sem.at[number, peer],
            recv_sem.at[number, peer], device_id=target(peer * team + member, hd_size),
            device_id_type=MESH,
        )

    def own(number):
        source, dest = arrays[number]
        return pltpu.make_async_copy(source.at[:, columns(head)], dest(head), own_sem.at[number])

    def shared(number, block, other, owner):
        ref = (k_out, v_out)[number]
        return pltpu.make_async_remote_copy(
            ref.at[block, owner], ref.at[block, owner], pass_send.at[number, block, other],
            pass_recv.at[number, block, owner], device_id=target(head * team + other, hd_size),
            device_id_type=MESH,
        )

    def share(number, block):
        @pl.loop(1, team)
        def _(step):
            shared(number, block, (member + step) % team, member).start()

    for number in range(4):
        own(number).start()

    for pair in ((0, 1), (2, 3)):
        @pl.loop(0, HEADS - 1)
        def _(step):
            peer = (head + far_first(step)) % HEADS
            for number in pair:
                remote(number, peer).start()

    for number in range(4):
        own(number).wait()
    for number in range(2):
        share(number, head)

    @pl.loop(0, HEADS - 1)
    def _(step):
        peer = (head + HEADS - far_first(step)) % HEADS
        for number in range(2):
            arrival(number, peer).wait_recv()
            share(number, peer)

    @pl.loop(0, HEADS - 1)
    def _(step):
        peer = (head + HEADS - far_first(step)) % HEADS
        for number in (2, 3):
            arrival(number, peer).wait_recv()

    @pl.loop(0, HEADS - 1)
    def _(step):
        peer = (head + far_first(step)) % HEADS
        for number in range(4):
            remote(number, peer).wait_send()

    @pl.loop(1, team)
    def _(step):
        other = (member + step) % team

        @pl.loop(0, HEADS)
        def _(block):
            for number in range(2):
                shared(number, block, other, member).wait_send()
                shared(number, block, other, other).wait_recv()


def dot(a, b, a_dim, b_dim):
    return lax.dot_general(
        a, b, (((a_dim,), (b_dim,)), ((), ())), preferred_element_type=jnp.float32
    )


def attention_kernel(team, hd_size, pattern, q_ref, g_ref, k_ref, v_ref, o_ref, dq_ref, dk_ref, dv_ref):
    _, member = place(team, hd_size)
    blocks = k_ref.shape[0]
    scale = 1.0 / math.sqrt(HEAD_DIM)

    @pl.loop(0, blocks)
    def _(at):
        dk_ref[at] = jnp.zeros((BLOCK, HEAD_DIM), jnp.float32)
        dv_ref[at] = jnp.zeros((BLOCK, HEAD_DIM), jnp.float32)

    def step(at):
        block = at * team + member
        left_ok, right_ok = block >= 1, block + 1 < blocks
        ids = [jnp.maximum(block - 1, 0), block, jnp.minimum(block + 1, blocks - 1)]
        ids += list(range(GLOBALS)) + [pattern[block, r] for r in range(RANDOM)]
        allowed = [left_ok, None, right_ok] + [None] * (GLOBALS + RANDOM)
        queries, cotangent = q_ref[at], g_ref[at]
        keys = jnp.concatenate([k_ref[i] for i in ids], axis=0)
        values = jnp.concatenate([v_ref[i] for i in ids], axis=0)
        scores = dot(keys, queries, 1, 1) * scale
        parts = []
        for entry, ok in enumerate(allowed):
            part = scores[entry * BLOCK : (entry + 1) * BLOCK]
            parts.append(part if ok is None else jnp.where(ok, part, MASK_VALUE))
        scores = jnp.concatenate(parts, axis=0)
        weights = jnp.exp(scores - jnp.max(scores, axis=0, keepdims=True))
        total = jnp.sum(weights, axis=0, keepdims=True)
        soft = (weights * (1.0 / total)).astype(jnp.bfloat16)
        prob_grad = dot(values, cotangent, 1, 1)
        wide = soft.astype(jnp.float32)
        delta = jnp.sum(wide * prob_grad, axis=0, keepdims=True)
        score_grad = (wide * ((prob_grad - delta) * scale)).astype(jnp.bfloat16)
        o_ref[at] = dot(soft, values, 0, 0).astype(o_ref.dtype)
        dq_ref[at] = dot(score_grad, keys, 0, 0).astype(dq_ref.dtype)
        key_terms = dot(score_grad, queries, 1, 0)
        value_terms = dot(soft, cotangent, 1, 0)
        for entry, i in enumerate(ids):
            rows = slice(entry * BLOCK, (entry + 1) * BLOCK)
            dk_ref[i] += key_terms[rows]
            dv_ref[i] += value_terms[rows]

    @pl.loop(0, HEADS)
    def _(at):
        step(at)


def scatter_kernel(
    team, hd_size, o_in, dq_in, dk_in, dv_in, o_out, dq_out, dk_out, dv_out,
    mine, theirs, summed, send_sem, recv_sem, own_sem, pass_send, pass_recv, load_sem,
):
    head, member = place(team, hd_size)
    parts = (dk_in, dv_in)
    arrays = (
        (lambda at: o_in.at[at], o_out),
        (lambda at: dq_in.at[at], dq_out),
        (lambda at: summed.at[0, at], dk_out),
        (lambda at: summed.at[1, at], dv_out),
    )

    def load(number):
        return pltpu.make_async_copy(
            parts[number].at[:, member], mine.at[number], load_sem.at[number]
        )

    for number in range(2):
        load(number).start()
    enter(head, member, team, hd_size)

    def shared(number, block, step, other):
        return pltpu.make_async_remote_copy(
            parts[number].at[block, other], theirs.at[step - 1, number, block],
            pass_send.at[step - 1, number, block], pass_recv.at[step - 1, number, block],
            device_id=target(head * team + other, hd_size), device_id_type=MESH,
        )

    def remote(number, peer):
        source, dest = arrays[number]
        return pltpu.make_async_remote_copy(
            source(peer), dest.at[:, columns(head)], send_sem.at[number, peer],
            recv_sem.at[number, head], device_id=target(peer * team + member, hd_size),
            device_id_type=MESH,
        )

    def arrival(number, peer):
        source, dest = arrays[number]
        return pltpu.make_async_remote_copy(
            source(peer), dest.at[:, columns(peer)], send_sem.at[number, peer],
            recv_sem.at[number, peer], device_id=target(peer * team + member, hd_size),
            device_id_type=MESH,
        )

    def own(number):
        source, dest = arrays[number]
        return pltpu.make_async_copy(source(head), dest.at[:, columns(head)], own_sem.at[number])

    @pl.loop(0, HEADS)
    def _(turn):
        block = (head + far_first(turn % (HEADS - 1)) * (1 - turn // (HEADS - 1))) % HEADS

        @pl.loop(1, team)
        def _(step):
            for number in range(2):
                shared(number, block, step, (member + step) % team).start()

    @pl.loop(0, HEADS - 1)
    def _(step):
        peer = (head + far_first(step)) % HEADS
        for number in range(2):
            remote(number, peer).start()

    for number in range(2):
        own(number).start()
    for number in range(2):
        load(number).wait()

    def add(block):
        @pl.loop(1, team)
        def _(step):
            for number in range(2):
                shared(number, block, step, (member + step) % team).wait_recv()
        for number in range(2):
            summed[number, block] = lax.fori_loop(
                0, team - 1, lambda step, total: total + theirs[step, number, block],
                mine[number, block],
            ).astype(summed.dtype)

    add((head + far_first(0)) % HEADS)

    @pl.loop(0, HEADS - 1)
    def _(step):
        later = step + 1
        add((head + far_first(later % (HEADS - 1)) * (1 - later // (HEADS - 1))) % HEADS)
        peer = (head + far_first(step)) % HEADS
        for number in (2, 3):
            remote(number, peer).start()

    for number in (2, 3):
        own(number).start()

    @pl.loop(0, HEADS - 1)
    def _(step):
        peer = (head + HEADS - far_first(step)) % HEADS
        for number in range(4):
            arrival(number, peer).wait_recv()

    @pl.loop(0, HEADS - 1)
    def _(step):
        peer = (head + far_first(step)) % HEADS
        for number in range(4):
            remote(number, peer).wait_send()

    @pl.loop(1, team)
    def _(step):
        @pl.loop(0, HEADS)
        def _(block):
            for number in range(2):
                shared(number, block, step, (member + step) % team).wait_send()

    for number in range(4):
        own(number).wait()


def on_device(query_states, key_states, value_states, output_cotangent, pattern):
    hd_size = lax.axis_size("hd")
    devices = lax.axis_size("grp") * hd_size
    team = devices // HEADS
    blocks = pattern.shape[0]
    bf16, f32 = jnp.bfloat16, jnp.float32
    dma = pltpu.SemaphoreType.DMA
    anywhere = pl.BlockSpec(memory_space=pl.ANY)
    vmem = pl.BlockSpec(memory_space=pltpu.VMEM)
    tile = (BLOCK, HEAD_DIM)
    own_shape = jax.ShapeDtypeStruct((HEADS, *tile), bf16)
    all_shape = jax.ShapeDtypeStruct((HEADS, team, *tile), bf16)
    part_shape = jax.ShapeDtypeStruct((blocks, *tile), f32)

    queries, keys, values, cotangent = pl.pallas_call(
        functools.partial(gather_kernel, team, hd_size),
        out_shape=(own_shape, all_shape, all_shape, own_shape),
        in_specs=[anywhere] * 4,
        out_specs=(anywhere,) * 4,
        scratch_shapes=[
            dma((4, HEADS)), dma((4, HEADS)), dma((4,)),
            dma((2, HEADS, team)), dma((2, HEADS, team)),
        ],
        compiler_params=pltpu.CompilerParams(collective_id=0, has_side_effects=True),
        name="gather_heads",
    )(query_states, key_states, value_states, output_cotangent)

    attended, query_grad, key_part, value_part = pl.pallas_call(
        functools.partial(attention_kernel, team, hd_size),
        out_shape=(own_shape, own_shape, part_shape, part_shape),
        in_specs=[pl.BlockSpec(memory_space=pltpu.SMEM)] + [vmem] * 4,
        out_specs=(vmem,) * 4,
        compiler_params=pltpu.CompilerParams(vmem_limit_bytes=VMEM_BYTES),
        name="attention",
    )(pattern, queries, cotangent, keys.reshape(blocks, *tile), values.reshape(blocks, *tile))

    out_shape = jax.ShapeDtypeStruct(query_states.shape, bf16)
    return pl.pallas_call(
        functools.partial(scatter_kernel, team, hd_size),
        out_shape=(out_shape,) * 4,
        in_specs=[anywhere] * 4,
        out_specs=(anywhere,) * 4,
        scratch_shapes=[
            pltpu.VMEM((2, HEADS, *tile), f32),
            pltpu.VMEM((team - 1, 2, HEADS, *tile), f32),
            pltpu.VMEM((2, HEADS, *tile), bf16),
            dma((4, HEADS)), dma((4, HEADS)), dma((4,)),
            dma((team - 1, 2, HEADS)), dma((team - 1, 2, HEADS)), dma((2,)),
        ],
        compiler_params=pltpu.CompilerParams(
            collective_id=1, has_side_effects=True, vmem_limit_bytes=VMEM_BYTES
        ),
        name="scatter_heads",
    )(
        attended, query_grad,
        key_part.reshape(HEADS, team, *tile), value_part.reshape(HEADS, team, *tile),
    )


def solution(mesh):
    split = P(("grp", "hd"), None)
    return jax.shard_map(
        on_device, mesh=mesh, in_specs=(split,) * 4 + (P(),), out_specs=(split,) * 4,
        check_vma=False,
    )
```

time: 530 us -> 136 us (0.26); the launches traced: 520 us -> 136 us
  waiting for transfers between devices: 250 us -> 0 us
  local copies, waits for them, and re-layouts: 148 us -> 6.81 us
  Pallas kernels: 0 us -> 128 us
  starting transfers between devices: 41.7 us -> 0 us
  matrix products: 34.3 us -> 0 us
  other arithmetic: 29.5 us -> 0 us
  between operations: 16.2 us -> 0.67 us
    all_to_all x10 -> x0, waiting for transfers between devices: 203 us -> none  [the longest x1 88.1 us: on_device(): lax.all_to_all(outgoing, 'grp', split_axis=0, concat_axis=0, tiled=True)]
    pallas_call x0 -> x3, Pallas kernels: none -> 128 us  [the longest x1 56.3 us: on_device(): pl.pallas_call(functools.partial(gather_kernel, team, hd_size), out_shape...]
    reshape x8 -> x0, local copies, waits for them, and re-layouts: 56 us -> none  [the longest x2 17.7 us: backward_step(): value_terms.reshape(step_blocks, key_count, BLOCK, head_width)]
    psum x2 -> x0, waiting for transfers between devices: 46.8 us -> none  [the longest x1 24.1 us: spread_2(): return lax.psum(jnp.where(mine, array, jnp.zeros_like(array)), axis)]
    all_to_all x10 -> x0, starting transfers between devices: 41.6 us -> none  [the longest x1 6.59 us: on_device(): lax.all_to_all(outgoing, 'grp', split_axis=0, concat_axis=0, tiled=True)]
    dot_general x9 -> x0, matrix products: 34.3 us -> none  [the longest x1 7.56 us: on_device(): jnp.einsum('gcj,gctx->jtx', selector, returned, preferred_element_type=jn...]
    scatter-add x3 -> x0, local copies, waits for them, and re-layouts: 30.4 us -> none  [the longest x2 22.1 us: on_device(): slot_sum = slot_sum.at[left_slot].add(window_terms[0, 0]).at[right_slot]....]
    slice x7 -> x0, local copies, waits for them, and re-layouts: 13.5 us -> none  [the longest x1 5.19 us: split_pairs(): pair_part[..., head_width:]]
  transfers between devices with their start and end apart: 12 -> 0, of which waited for: 9 -> 0; matrix products, arithmetic and copies ran while one was open for 16% -> 0% of each run, Pallas kernels for 0% -> 0%
where the time goes in v1:
time: 136 us
  Pallas kernels  128 us (94%)
  local copies, waits for them, and re-layouts  6.81 us (5%)
    pallas_call x1, Pallas kernels, on_device(): pl.pallas_call(functools.partial(gather_kernel, team, hd_size), out_shape...  56.3 us
    pallas_call x1, Pallas kernels, on_device(): pl.pallas_call(functools.partial(scatter_kernel, team, hd_size), out_shap...  52.3 us
    pallas_call x1, Pallas kernels, on_device(): pl.pallas_call(functools.partial(attention_kernel, team, hd_size), out_sh...  19.7 us
    unnamed x9, local copies, waits for them, and re-layouts  6.81 us

profile of v1, /device:TPU:0, one launch (start us, length us, event | category | flops | bytes accessed | tf_op | source)
XLA Modules:
  0.0 135.7 jit_solution(1032077429852374458)
XLA Ops:
  0.6 1.4 %copy.9.pattern = s32[32,2]{1,0:T(8,128)} copy(s32[32,2]{0,1:T(2,128)} %param.9) | data formatting | bytes 512 | tf_op args[4]
  2.0 56.3 %gather_heads.1 = (bf16[16,128,128]{2,1,0:T(8,128)(2,1)}, bf16[16,2,128,128]{3,2,1,0:T(8,128)(2,1)}, bf16[16,2,128,128]{3,2,1,0:T(8,128)(2,1)}, bf16[16,128,128]{2,1,0:T(8,128)(2,1)}) custom-call(bf16[128,2048]{1,0:T(8,128)(2,1)} %q_in.1, bf16[128,2048]{1,0:T(8,128)(2,1)} %k_in.1, bf16[128,2048]{1,0:T(8,128)(2,1)} %v_in.1, bf16[128,2048]{1,0:T(8,128)(2,1)} %g_in.1), custom_call_target="tpu_custom_call" | custom-call | tf_op jit(solution)/shard_map/gather_heads/pallas_call | solution.py:328
  58.3 19.7 %attention.1 = (bf16[16,128,128]{2,1,0:T(8,128)(2,1)}, bf16[16,128,128]{2,1,0:T(8,128)(2,1)}, f32[32,128,128]{2,1,0:T(8,128)}, f32[32,128,128]{2,1,0:T(8,128)}) custom-call(s32[32,2]{1,0:T(8,128)} %copy.9.pattern, bf16[16,128,128]{2,1,0:T(8,128)(2,1)} %get-tuple-element.12.q_ref, bf16[16,128,128]{2,1,0:T(8,128)(2,1)} %get-tuple-element.13.g_ref, ...), custom_call_target="tpu_custom_call" | custom-call | tf_op jit(solution)/shard_map/attention/pallas_call | solution.py:341
  78.0 52.3 %scatter_heads.1 = (bf16[128,2048]{1,0:T(8,128)(2,1)}, bf16[128,2048]{1,0:T(8,128)(2,1)}, bf16[128,2048]{1,0:T(8,128)(2,1)}, bf16[128,2048]{1,0:T(8,128)(2,1)}) custom-call(bf16[16,128,128]{2,1,0:T(8,128)(2,1)} %get-tuple-element.16.o_in, bf16[16,128,128]{2,1,0:T(8,128)(2,1)} %get-tuple-element.17.dq_in, f32[16,2,128,128]{3,2,1,0:T(8,128)} %bitcast.4, ...), custom_call_target="tpu_custom_call" | custom-call | tf_op jit(solution)/shard_map/scatter_heads/pallas_call | solution.py:351
  130.3 0.0 copy-start.1
  130.3 0.0 copy-start
  130.3 2.0 %copy.14 = bf16[128,2048]{1,0:T(8,128)(2,1)} copy(bf16[128,2048]{1,0:T(8,128)(2,1)} %get-tuple-element.24) | data formatting | bytes 1048576
  132.3 1.9 %copy.15 = bf16[128,2048]{1,0:T(8,128)(2,1)} copy(bf16[128,2048]{1,0:T(8,128)(2,1)} %get-tuple-element.25) | data formatting | bytes 1048576
  134.1 0.0 copy-done.1
  134.1 0.8 copy.16
  134.9 0.0 copy-done
  134.9 0.8 copy.17
Async XLA Ops:
  130.3 3.9 %copy-start.1 = (bf16[128,2048]{1,0:T(8,128)(2,1)S(1)}, bf16[128,2048]{1,0:T(8,128)(2,1)}, u32[]{:S(2)}) copy-start(bf16[128,2048]{1,0:T(8,128)(2,1)} %get-tuple-element.26) | copy-start | bytes 1572868
  130.3 4.7 %copy-start = (bf16[128,2048]{1,0:T(8,128)(2,1)S(1)}, bf16[128,2048]{1,0:T(8,128)(2,1)}, u32[]{:S(2)}) copy-start(bf16[128,2048]{1,0:T(8,128)(2,1)} %get-tuple-element.27) | copy-start | bytes 1572868

commit v2 on v1

v2 whole, which is shorter than its diff:
```python
import functools
import math

import jax
import jax.numpy as jnp
from jax import lax
from jax.experimental import pallas as pl
from jax.experimental.pallas import tpu as pltpu
from jax.sharding import PartitionSpec as P

HEADS = 16
HEAD_DIM = 128
BLOCK = 128
GLOBALS = 1
RANDOM = 2
MASK_VALUE = -1e30
VMEM_BYTES = 60 * 1024 * 1024
MESH = pl.DeviceIdType.MESH


def place(team, hd_size):
    index = lax.axis_index("grp") * hd_size + lax.axis_index("hd")
    return index // team, index % team


def target(number, hd_size):
    return (number // hd_size, number % hd_size)


def offset(turn):
    return (1 + (HEADS // 2 - 2 + turn) % (HEADS - 1)) * ((turn + HEADS - 1) // HEADS)


def enter(head, member, team, hd_size):
    barrier = pltpu.get_barrier_semaphore()

    def greet(number):
        pl.semaphore_signal(barrier, inc=1, device_id=target(number, hd_size), device_id_type=MESH)

    @pl.loop(1, HEADS)
    def _(step):
        greet((head + step) % HEADS * team + member)

    @pl.loop(1, team)
    def _(step):
        greet(head * team + (member + step) % team)

    pl.semaphore_wait(barrier, HEADS - 1 + team - 1)


def columns(head):
    return pl.ds(pl.multiple_of(head * HEAD_DIM, HEAD_DIM), HEAD_DIM)


def dot(a, b, a_dim, b_dim):
    return lax.dot_general(
        a, b, (((a_dim,), (b_dim,)), ((), ())), preferred_element_type=jnp.float32
    )


def kernel(
    team, hd_size, pattern, q_in, k_in, v_in, g_in, o_out, dq_out, dk_out, dv_out,
    q_buf, g_buf, k_buf, v_buf, o_buf, dq_buf, window, chain, shared_sum, stage, theirs, summed,
    previous, latest, in_send, in_recv, in_own, pass_send, pass_recv,
    out_send, out_recv, out_own, team_send, team_recv,
):
    head, member = place(team, hd_size)
    blocks = k_buf.shape[0]
    scale = 1.0 / math.sqrt(HEAD_DIM)
    ins = (
        (k_in, lambda at: k_buf.at[at * team + member]),
        (v_in, lambda at: v_buf.at[at * team + member]),
        (q_in, lambda at: q_buf.at[at]),
        (g_in, lambda at: g_buf.at[at]),
    )
    outs = (
        (lambda at: o_buf.at[at], o_out),
        (lambda at: dq_buf.at[at], dq_out),
        (lambda at: summed.at[0, at], dk_out),
        (lambda at: summed.at[1, at], dv_out),
    )

    def receiver(turn):
        return (head + offset(turn)) % HEADS

    def sender(turn):
        return (head + HEADS - offset(turn)) % HEADS

    def in_copy(number, peer, lands):
        source, dest = ins[number]
        return pltpu.make_async_remote_copy(
            source.at[:, columns(peer)], dest(lands), in_send.at[number, peer],
            in_recv.at[number, lands], device_id=target(peer * team + member, hd_size),
            device_id_type=MESH,
        )

    def in_local(number):
        source, dest = ins[number]
        return pltpu.make_async_copy(source.at[:, columns(head)], dest(head), in_own.at[number])

    def pass_copy(number, at, other, owner):
        ref = (k_buf, v_buf)[number].at[at * team + owner]
        return pltpu.make_async_remote_copy(
            ref, ref, pass_send.at[number, at, other], pass_recv.at[number, at, owner],
            device_id=target(head * team + other, hd_size), device_id_type=MESH,
        )

    def out_copy(number, peer, lands):
        source, dest = outs[number]
        return pltpu.make_async_remote_copy(
            source(peer), dest.at[:, columns(lands)], out_send.at[number, peer],
            out_recv.at[number, lands], device_id=target(peer * team + member, hd_size),
            device_id_type=MESH,
        )

    def out_local(number):
        source, dest = outs[number]
        return pltpu.make_async_copy(source(head), dest.at[:, columns(head)], out_own.at[number])

    def team_copy(number, at, step):
        return pltpu.make_async_remote_copy(
            stage.at[step - 1, number, at], theirs.at[step - 1, number, at],
            team_send.at[step - 1, number, at], team_recv.at[step - 1, number, at],
            device_id=target(head * team + (member + step) % team, hd_size), device_id_type=MESH,
        )

    def share(number, at):
        @pl.loop(1, team)
        def _(step):
            pass_copy(number, at, (member + step) % team, member).start()

    for number in range(4):
        in_local(number).start()
    enter(head, member, team, hd_size)

    for pair in ((0, 1), (2, 3)):
        @pl.loop(1, HEADS)
        def _(turn):
            peer = receiver(turn)
            for number in pair:
                in_copy(number, peer, head).start()

    for number in range(4):
        in_local(number).wait()
    for number in range(2):
        share(number, head)

    names = [
        pattern[sender(turn) * team + member, r] for turn in range(HEADS) for r in range(RANDOM)
    ]
    for later in range(len(names)):
        found = jnp.int32(-1)
        for earlier in range(later):
            found = jnp.where(names[earlier] == names[later], earlier, found)
        previous[later] = found

    @pl.loop(0, blocks)
    def _(block):
        found = jnp.int32(-1)
        for entry, name in enumerate(names):
            found = jnp.where(name == block, entry, found)
        latest[block] = found

    zeros = jnp.zeros((BLOCK, HEAD_DIM), jnp.float32)
    for number in range(2):
        shared_sum[number] = zeros
        for role in (0, 2):
            for at in (0, HEADS + 1):
                window[number, role, at] = zeros.astype(window.dtype)

    @pl.loop(1, HEADS)
    def _(turn):
        peer = sender(turn)
        for number in range(2):
            in_copy(number, head, peer).wait_recv()
            share(number, peer)

    @pl.loop(1, team)
    def _(step):
        other = (member + step) % team

        @pl.loop(0, HEADS)
        def _(turn):
            at = sender(turn)
            for number in range(2):
                pass_copy(number, at, other, other).wait_recv()

    def attend(turn, at):
        block = at * team + member
        ids = [jnp.maximum(block - 1, 0), block, jnp.minimum(block + 1, blocks - 1)]
        ids += list(range(GLOBALS)) + [pattern[block, r] for r in range(RANDOM)]
        allowed = [block >= 1, None, block + 1 < blocks] + [None] * (GLOBALS + RANDOM)
        queries, cotangent = q_buf[at], g_buf[at]
        keys = jnp.concatenate([k_buf[i] for i in ids], axis=0)
        values = jnp.concatenate([v_buf[i] for i in ids], axis=0)
        scores = dot(keys, queries, 1, 1) * scale
        parts = []
        for entry, ok in enumerate(allowed):
            part = scores[entry * BLOCK : (entry + 1) * BLOCK]
            parts.append(part if ok is None else jnp.where(ok, part, MASK_VALUE))
        scores = jnp.concatenate(parts, axis=0)
        weights = jnp.exp(scores - jnp.max(scores, axis=0, keepdims=True))
        total = jnp.sum(weights, axis=0, keepdims=True)
        soft = (weights * (1.0 / total)).astype(jnp.bfloat16)
        prob_grad = dot(values, cotangent, 1, 1)
        wide = soft.astype(jnp.float32)
        delta = jnp.sum(wide * prob_grad, axis=0, keepdims=True)
        score_grad = (wide * ((prob_grad - delta) * scale)).astype(jnp.bfloat16)
        o_buf[at] = dot(soft, values, 0, 0).astype(o_buf.dtype)
        dq_buf[at] = dot(score_grad, keys, 0, 0).astype(dq_buf.dtype)
        terms = (dot(score_grad, queries, 1, 0), dot(soft, cotangent, 1, 0))
        for number, term in enumerate(terms):
            entries = [term[e * BLOCK : (e + 1) * BLOCK] for e in range(len(ids))]
            for role in range(3):
                window[number, role, at + 1] = entries[role].astype(window.dtype)
            shared_sum[number] += entries[3]
            for r in range(RANDOM):
                slot = turn * RANDOM + r
                before = previous[slot]
                held = chain[number, jnp.maximum(before, 0)]
                chain[number, slot] = entries[3 + GLOBALS + r] + jnp.where(before >= 0, held, 0.0)

    @pl.loop(0, HEADS)
    def _(turn):
        at = sender(turn)

        @pl.when(turn > 0)
        def _():
            for number in (2, 3):
                in_copy(number, head, at).wait_recv()

        attend(turn, at)

        @pl.when(turn > 1)
        def _():
            before = sender(turn - 1)
            for number in range(2):
                out_copy(number, before, head).start()

    def base(number, block):
        last = latest[block]
        total = jnp.where(last >= 0, chain[number, jnp.maximum(last, 0)], 0.0)
        return total + jnp.where(block == 0, shared_sum[number], 0.0)

    def prepare(at, step):
        block = at * team + (member + step) % team
        for number in range(2):
            total = base(number, block)
            right = window[number, 2, at + 1 - (member + 1) // team].astype(jnp.float32)
            left = window[number, 0, at + 1 + (team - member) // team].astype(jnp.float32)
            total += jnp.where(step == 1, right, 0.0) + jnp.where(step == team - 1, left, 0.0)
            stage[step - 1, number, at] = total.astype(stage.dtype)

    last_peer = sender(HEADS - 1)
    for number in range(2):
        out_copy(number, last_peer, head).start()
        out_local(number).start()

    @pl.loop(1, HEADS + 2)
    def _(turn):
        @pl.when(turn <= HEADS)
        def _():
            @pl.loop(1, team)
            def _(step):
                prepare(receiver(turn % HEADS), step)

        @pl.when(turn > 1)
        def _():
            @pl.loop(1, team)
            def _(step):
                for number in range(2):
                    team_copy(number, receiver((turn - 1) % HEADS), step).start()

    @pl.loop(1, HEADS + 1)
    def _(turn):
        at = receiver(turn % HEADS)

        @pl.loop(1, team)
        def _(step):
            for number in range(2):
                team_copy(number, at, step).wait_recv()

        for number in range(2):
            own = base(number, at * team + member)
            own += window[number, 1, at + 1].astype(jnp.float32)
            summed[number, at] = lax.fori_loop(
                0, team - 1,
                lambda step, total: total + theirs[step, number, at].astype(jnp.float32), own,
            ).astype(summed.dtype)

        @pl.when(turn > 1)
        def _():
            for number in (2, 3):
                out_copy(number, receiver(turn - 1), head).start()

    for number in (2, 3):
        out_local(number).start()

    @pl.loop(1, HEADS)
    def _(turn):
        to, source = receiver(turn), sender(turn)
        for number in range(4):
            in_copy(number, to, head).wait_send()
            out_copy(number, to, head).wait_send()
            out_copy(number, head, source).wait_recv()

    @pl.loop(1, team)
    def _(step):
        @pl.loop(0, HEADS)
        def _(at):
            for number in range(2):
                pass_copy(number, at, (member + step) % team, member).wait_send()
                team_copy(number, at, step).wait_send()

    for number in range(4):
        out_local(number).wait()


def on_device(query_states, key_states, value_states, output_cotangent, pattern):
    hd_size = lax.axis_size("hd")
    devices = lax.axis_size("grp") * hd_size
    team = devices // HEADS
    blocks = pattern.shape[0]
    bf16, f32 = jnp.bfloat16, jnp.float32
    dma = pltpu.SemaphoreType.DMA
    anywhere = pl.BlockSpec(memory_space=pl.ANY)
    tile = (BLOCK, HEAD_DIM)
    out_shape = jax.ShapeDtypeStruct(query_states.shape, bf16)
    return pl.pallas_call(
        functools.partial(kernel, team, hd_size),
        out_shape=(out_shape,) * 4,
        in_specs=[pl.BlockSpec(memory_space=pltpu.SMEM)] + [anywhere] * 4,
        out_specs=(anywhere,) * 4,
        scratch_shapes=[
            pltpu.VMEM((HEADS, *tile), bf16),
            pltpu.VMEM((HEADS, *tile), bf16),
            pltpu.VMEM((blocks, *tile), bf16),
            pltpu.VMEM((blocks, *tile), bf16),
            pltpu.VMEM((HEADS, *tile), bf16),
            pltpu.VMEM((HEADS, *tile), bf16),
            pltpu.VMEM((2, 3, HEADS + 2, *tile), bf16),
            pltpu.VMEM((2, HEADS * RANDOM, *tile), f32),
            pltpu.VMEM((2, *tile), f32),
            pltpu.VMEM((team - 1, 2, HEADS, *tile), bf16),
            pltpu.VMEM((team - 1, 2, HEADS, *tile), bf16),
            pltpu.VMEM((2, HEADS, *tile), bf16),
            pltpu.SMEM((HEADS * RANDOM,), jnp.int32),
            pltpu.SMEM((blocks,), jnp.int32),
            dma((4, HEADS)), dma((4, HEADS)), dma((4,)),
            dma((2, HEADS, team)), dma((2, HEADS, team)),
            dma((4, HEADS)), dma((4, HEADS)), dma((4,)),
            dma((team - 1, 2, HEADS)), dma((team - 1, 2, HEADS)),
        ],
        compiler_params=pltpu.CompilerParams(
            collective_id=0, has_side_effects=True, vmem_limit_bytes=VMEM_BYTES
        ),
        name="head_attention",
    )(pattern, query_states, key_states, value_states, output_cotangent)


def solution(mesh):
    split = P(("grp", "hd"), None)
    return jax.shard_map(
        on_device, mesh=mesh, in_specs=(split,) * 4 + (P(),), out_specs=(split,) * 4,
        check_vma=False,
    )
```

time: 136 us -> 112 us (0.82)
  Pallas kernels: 128 us -> 104 us
    pallas_call x3 -> x1, Pallas kernels: 128 us -> 104 us  [on_device(): pl.pallas_call(functools.partial(kernel, team, hd_size), out_shape=(out_s...]
    unnamed x9 -> x11, local copies, waits for them, and re-layouts: 6.81 us -> 6.56 us
where the time goes in v2:
time: 112 us; the launch traced here: 111 us
  Pallas kernels  104 us (93%)
  local copies, waits for them, and re-layouts  6.56 us (6%)
    pallas_call x1, Pallas kernels, on_device(): pl.pallas_call(functools.partial(kernel, team, hd_size), out_shape=(out_s...  104 us
    unnamed x11, local copies, waits for them, and re-layouts  6.56 us

profile of v2, /device:TPU:0, one launch (start us, length us, event | category | flops | bytes accessed | tf_op | source)
XLA Modules:
  0.0 111.4 jit_solution(11262506120737874739)
XLA Ops:
  0.6 1.4 %copy.9.pattern = s32[32,2]{1,0:T(8,128)} copy(s32[32,2]{0,1:T(2,128)} %param.9) | data formatting | bytes 512 | tf_op args[4]
  2.0 104.2 %head_attention.1 = (bf16[128,2048]{1,0:T(8,128)(2,1)}, bf16[128,2048]{1,0:T(8,128)(2,1)}, bf16[128,2048]{1,0:T(8,128)(2,1)}, bf16[128,2048]{1,0:T(8,128)(2,1)}) custom-call(s32[32,2]{1,0:T(8,128)} %copy.9.pattern, bf16[128,2048]{1,0:T(8,128)(2,1)} %q_in.1, bf16[128,2048]{1,0:T(8,128)(2,1)} %k_in.1, bf16[128,2048]{1,0:T(8,128)(2,1)} %v_in.1, ...), custom_call_target="tpu_custom_call" | custom-call | tf_op jit(solution)/shard_map/head_attention/pallas_call | solution.py:329
  106.2 0.0 copy-start.2
  106.2 1.9 %copy.14 = bf16[128,2048]{1,0:T(8,128)(2,1)} copy(bf16[128,2048]{1,0:T(8,128)(2,1)} %get-tuple-element.8) | data formatting | bytes 1048576
  108.1 0.0 copy-done.2
  108.1 0.0 copy-start.1
  108.1 0.8 copy.15
  108.9 0.4 copy-done.1
  109.3 0.0 copy-start
  109.3 0.8 copy.16
  110.1 0.4 copy-done
  110.6 0.8 copy.17
Async XLA Ops:
  106.2 2.0 %copy-start.2 = (bf16[128,2048]{1,0:T(8,128)(2,1)S(1)}, bf16[128,2048]{1,0:T(8,128)(2,1)}, u32[]{:S(2)}) copy-start(bf16[128,2048]{1,0:T(8,128)(2,1)} %get-tuple-element.9) | copy-start | bytes 1572868
  108.1 1.2 %copy-start.1 = (bf16[128,2048]{1,0:T(8,128)(2,1)S(1)}, bf16[128,2048]{1,0:T(8,128)(2,1)}, u32[]{:S(2)}) copy-start(bf16[128,2048]{1,0:T(8,128)(2,1)} %get-tuple-element.10) | copy-start | bytes 1572868
  109.3 1.2 %copy-start = (bf16[128,2048]{1,0:T(8,128)(2,1)S(1)}, bf16[128,2048]{1,0:T(8,128)(2,1)}, u32[]{:S(2)}) copy-start(bf16[128,2048]{1,0:T(8,128)(2,1)} %get-tuple-element.11) | copy-start | bytes 1572868

commit v3 on v2

--- a/solution.py
+++ b/solution.py
@@ -27,8 +27,15 @@
     return (number // hd_size, number % hd_size)
 
 
-def offset(turn):
-    return (1 + (HEADS // 2 - 2 + turn) % (HEADS - 1)) * ((turn + HEADS - 1) // HEADS)
+def flip(number, mask, bit):
+    a, b = number // bit % 2, mask // bit % 2
+    return bit * ((a + b) % 2)
+
+
+def partner(head, turn):
+    far, near = turn % 4, turn // 4
+    mask = (far // 2 * 2 + (far % 2 + far // 2) % 2) * (HEADS // 4) + near
+    return sum(flip(head, mask, bit) for bit in (1, 2, 4, 8))
 
 
 def enter(head, member, team, hd_size):
@@ -81,10 +88,9 @@
     )
 
     def receiver(turn):
-        return (head + offset(turn)) % HEADS
-
-    def sender(turn):
-        return (head + HEADS - offset(turn)) % HEADS
+        return partner(head, turn)
+
+    sender = receiver
 
     def in_copy(number, peer, lands):
         source, dest = ins[number]
@@ -146,7 +152,7 @@
         share(number, head)
 
     names = [
-        pattern[sender(turn) * team + member, r] for turn in range(HEADS) for r in range(RANDOM)
+        pattern[r, sender(turn) * team + member] for turn in range(HEADS) for r in range(RANDOM)
     ]
     for later in range(len(names)):
         found = jnp.int32(-1)
@@ -188,7 +194,7 @@
     def attend(turn, at):
         block = at * team + member
         ids = [jnp.maximum(block - 1, 0), block, jnp.minimum(block + 1, blocks - 1)]
-        ids += list(range(GLOBALS)) + [pattern[block, r] for r in range(RANDOM)]
+        ids += list(range(GLOBALS)) + [pattern[r, block] for r in range(RANDOM)]
         allowed = [block >= 1, None, block + 1 < blocks] + [None] * (GLOBALS + RANDOM)
         queries, cotangent = q_buf[at], g_buf[at]
         keys = jnp.concatenate([k_buf[i] for i in ids], axis=0)
@@ -316,6 +322,19 @@
         out_local(number).wait()
 
 
+def finish(*refs):
+    ins, outs, held, loaded, stored = refs[:4], refs[4:8], refs[8], refs[9], refs[10]
+    loads = [pltpu.make_async_copy(ins[i], held.at[i], loaded.at[i]) for i in range(4)]
+    stores = [pltpu.make_async_copy(held.at[i], outs[i], stored.at[i]) for i in range(4)]
+    for load in loads:
+        load.start()
+    for load, store in zip(loads, stores):
+        load.wait()
+        store.start()
+    for store in stores:
+        store.wait()
+
+
 def on_device(query_states, key_states, value_states, output_cotangent, pattern):
     hd_size = lax.axis_size("hd")
     devices = lax.axis_size("grp") * hd_size
@@ -326,7 +345,7 @@
     anywhere = pl.BlockSpec(memory_space=pl.ANY)
     tile = (BLOCK, HEAD_DIM)
     out_shape = jax.ShapeDtypeStruct(query_states.shape, bf16)
-    return pl.pallas_call(
+    results = pl.pallas_call(
         functools.partial(kernel, team, hd_size),
         out_shape=(out_shape,) * 4,
         in_specs=[pl.BlockSpec(memory_space=pltpu.SMEM)] + [anywhere] * 4,
@@ -355,7 +374,15 @@
             collective_id=0, has_side_effects=True, vmem_limit_bytes=VMEM_BYTES
         ),
         name="head_attention",
-    )(pattern, query_states, key_states, value_states, output_cotangent)
+    )(pattern.T, query_states, key_states, value_states, output_cotangent)
+    return pl.pallas_call(
+        finish,
+        out_shape=(out_shape,) * 4,
+        in_specs=[anywhere] * 4,
+        out_specs=(anywhere,) * 4,
+        scratch_shapes=[pltpu.VMEM((4, *query_states.shape), bf16), dma((4,)), dma((4,))],
+        name="finish",
+    )(*results)
 
 
 def solution(mesh):

time: 112 us -> 107 us (0.955)
  local copies, waits for them, and re-layouts: 6.56 us -> 0 us
  Pallas kernels: 104 us -> 106 us
    unnamed x11 -> x0, local copies, waits for them, and re-layouts: 6.56 us -> none
    pallas_call x0 -> x1, Pallas kernels: none -> 2.42 us  [on_device(): pl.pallas_call(finish, out_shape=(out_shape,) * 4, in_specs=[anywhere] *...]
where the time goes in v3:
time: 107 us
  Pallas kernels  106 us (99%)
    pallas_call x1, Pallas kernels, on_device(): pl.pallas_call(functools.partial(kernel, team, hd_size), out_shape=(out_s...  104 us
    pallas_call x1, Pallas kernels, on_device(): pl.pallas_call(finish, out_shape=(out_shape,) * 4, in_specs=[anywhere] *...  2.42 us

profile of v3, /device:TPU:0, one launch (start us, length us, event | category | flops | bytes accessed | tf_op | source)
XLA Modules:
  0.0 106.6 jit_solution(13531695978604658892)
XLA Ops:
  0.6 103.6 %head_attention.1 = (bf16[128,2048]{1,0:T(8,128)(2,1)}, bf16[128,2048]{1,0:T(8,128)(2,1)}, bf16[128,2048]{1,0:T(8,128)(2,1)}, bf16[128,2048]{1,0:T(8,128)(2,1)}) custom-call(s32[2,32]{1,0:T(2,128)} %bitcast.1, bf16[128,2048]{1,0:T(8,128)(2,1)} %q_in.1, bf16[128,2048]{1,0:T(8,128)(2,1)} %k_in.1, bf16[128,2048]{1,0:T(8,128)(2,1)} %v_in.1, bf16[128,2048]{1,0:T(8,128)(2,1)} %g_in.1), custom_call_target="tpu_custom_call" | custom-call | tf_op jit(solution)/shard_map/head_attention/pallas_call | solution.py:348
  104.2 2.4 %finish.1 = (bf16[128,2048]{1,0:T(8,128)(2,1)}, bf16[128,2048]{1,0:T(8,128)(2,1)}, bf16[128,2048]{1,0:T(8,128)(2,1)}, bf16[128,2048]{1,0:T(8,128)(2,1)}) custom-call(bf16[128,2048]{1,0:T(8,128)(2,1)} %get-tuple-element.8.refs_0_, bf16[128,2048]{1,0:T(8,128)(2,1)} %get-tuple-element.9.refs_1_, bf16[128,2048]{1,0:T(8,128)(2,1)} %get-tuple-element.10.refs_2_, ...), custom_call_target="tpu_custom_call" | custom-call | tf_op jit(solution)/shard_map/finish/pallas_call | solution.py:378
